TPU v7x, 32 devices: a whole 2x2x4 slice. The times are simulated.
32 devices in a mesh: gx: 4 (over z), gy: 4 (over y, x), gz: 2 (over core).
Axes of the slice: x: 2, y: 2, z: 4, core: 2. Of those that a mesh axis runs over, the one named last changes fastest.
Arguments:
- e_field: float32 [3, 8, 128, 512], P(None, 'gz', 'gx', 'gy'), may hold values from -6 to 6
- h_field: float32 [3, 8, 128, 512], P(None, 'gz', 'gx', 'gy'), may hold values from -6 to 6
- pole_current: float32 [3, 8, 128, 512], P(None, 'gz', 'gx', 'gy'), may hold values from -6 to 6
- material: int32 [8, 128, 512], P('gz', 'gx', 'gy'), may hold values from 0 to 3
- pole_table: float32 [3, 4], replicated, may hold values from 0.2 to 0.9
- cotangent: float32 [16, 8, 4096], P(None, None, ('gx', 'gy', 'gz')), may hold values from -6 to 6
- cosines: float32 [2, 4096], P(None, ('gx', 'gy', 'gz')), may hold values from -0.7 to 0.7
- wavenumber: float32 [16], replicated, may hold values from 0.6 to 0.8
- time_phase: float32 [16], replicated, may hold values from -3.140625 to 3.140625
Outputs:
- e_next: float32 [3, 8, 128, 512], P(None, 'gz', 'gx', 'gy')
- h_next: float32 [3, 8, 128, 512], P(None, 'gz', 'gx', 'gy')
- pole_next: float32 [3, 8, 128, 512], P(None, 'gz', 'gx', 'gy')
All inputs are finite; a program needn't handle non-finite values.
Results may differ from a plain program's by a relative error of at most 0.0003.
Values sent between devices are 32-bit elements; how exact they have to be, the bound alone decides.
No kernel may reach another device: no remote copies, remote signals or barrier semaphores. Data moves between devices by JAX's collectives and lax.ppermute only.
A program may use at most 64 MiB of HBM per device.

v0:
```python
import math

import jax
import jax.numpy as jnp
from jax import lax
from jax.experimental import pallas as pl
from jax.experimental.pallas import tpu as pltpu
from jax.sharding import PartitionSpec as P


NPOLE = 4
LANES = 128


courant = 0.5


def exchange(array, axis, mask):
    return lax.ppermute(array, axis, [(i, i ^ mask) for i in range(lax.axis_size(axis))])


def gray(index):
    return index ^ (index >> 1)


def bits_of(size):
    return size.bit_length() - 1


def cmul(a, b):
    return (a[0] * b[0] - a[1] * b[1], a[0] * b[1] + a[1] * b[0])


def small_turn(angle):
    q = angle * angle
    c = 1.0 + q * (-1 / 2 + q * (1 / 24 + q * (-1 / 720 + q * (1 / 40320))))
    s = angle * (1.0 + q * (-1 / 6 + q * (1 / 120 + q * (-1 / 5040 + q * (1 / 362880)))))
    return c, s


def doubled(turn):
    c, s = turn
    return (c - s) * (c + s), 2.0 * (c * s)


def tree_levels(rows):
    levels = 0
    while 3 ** (levels + 1) * 8 <= rows:
        levels += 1
    return levels


def turn_table(first, unit, rows):
    powers = [unit]
    for _ in range(2):
        powers.append(doubled(powers[-1]))
    step = doubled(powers[-1])
    for level in range(max(1, tree_levels(rows))):
        powers.append(step)
        if level < tree_levels(rows):
            first = cmul(first, step)
        step = cmul(step, doubled(step))
    return [first, *powers]


def turn_count(rows):
    return 4 + max(1, tree_levels(rows))


def both_ways(value, turn):
    cc, ss = value[0] * turn[0], value[1] * turn[1]
    cs, sc = value[0] * turn[1], value[1] * turn[0]
    return (cc - ss, sc + cs), (cc + ss, sc - cs)


def rotations(table, rows):
    base, powers = table[0], table[1:]
    sub = lax.broadcasted_iota(jnp.int32, (8, base[0].shape[-1]), 0)
    value = tuple(jnp.broadcast_to(part, sub.shape) for part in base)
    for k in range(3):
        picked = (sub & (1 << k)) != 0
        value = cmul(value, (jnp.where(picked, powers[k][0], 1.0), jnp.where(picked, powers[k][1], 0.0)))
    blocks = [value]
    last = 0
    for level in range(tree_levels(rows)):
        last = level
        pairs = [both_ways(block, powers[3 + level]) for block in blocks]
        blocks = [pair[1] for pair in pairs] + blocks + [pair[0] for pair in pairs]
    while len(blocks) * 8 < rows:
        blocks.append(cmul(blocks[len(blocks) - 3**last], powers[3 + last]))
    return tuple(jnp.concatenate([block[i] for block in blocks], axis=0)[:rows] for i in (0, 1))


def split(value):
    high = value.astype(jnp.bfloat16)
    return high, (value - high.astype(jnp.float32)).astype(jnp.bfloat16)


def dot_nt(a, b):
    return lax.dot_general(a, b, (((1,), (1,)), ((), ())), preferred_element_type=jnp.float32)


def source_kernel(freqs, depth, wx, half, sizes, zslots, xslots, scale, zbits, closing):
    sx, sy, _ = sizes
    per = 4 // zslots
    main = 4 * xslots * wx

    def body(*refs):
        waves, packed = refs[:2]
        if closing:
            old_even, old_odd = refs[2:4]
            keep, send, xback, xturn, yturn, acc_even, acc_odd = refs[4 + zbits :]
        else:
            e_in, h_in, acc_even, acc_odd, e_near, h_near, xback, xturn, yturn, sems = refs[2:]
            copies = [
                pltpu.make_async_copy(source, target, sems.at[i])
                for i, (source, target) in enumerate(((e_in, e_near), (h_in, h_near)))
            ]
            for copy in copies:
                copy.start()
        ix, iy, iz = (lax.axis_index(name) for name in ("gx", "gy", "gz"))
        xbit, ybit, zbit = bits_of(sx), bits_of(sy), bits_of(zslots)
        starts = []
        for slot in range(xslots):
            code = ix
            for k in range(1, xbit):
                code = code ^ (((slot >> (xbit - 1 - k)) & 1) << k)
            starts.append((code * wx).astype(jnp.float32))
        zcode = 0
        for k in range(zbit):
            zcode = zcode * 2 + ((gray(iz) >> k) & 1)
        ycode = gray(iy)
        center = (2 * half - 1) / 2.0
        wave, phase = waves[0], waves[1]
        along_x = wave * packed[freqs, 0:1, :]
        along_y = wave * packed[freqs, 1:2, :]
        origin = along_y * center - phase
        unit = doubled(small_turn(0.5 * along_x))
        for xr in range(xslots):
            angle = along_x * starts[xr] + origin
            first = jnp.cos(angle), jnp.sin(angle)
            xback[xr, 0], xback[xr, 1] = cmul(first, (unit[0], -unit[1]))
            for k, turn in enumerate(turn_table(first, unit, wx)):
                xturn[xr, k, 0], xturn[xr, k, 1] = turn
        first = small_turn(0.5 * along_y)
        for k, turn in enumerate(turn_table(first, doubled(first), half)):
            yturn[k, 0], yturn[k, 1] = turn
        if closing:
            acc_even[...] = old_even[...]
            acc_odd[...] = old_odd[...]
        else:
            acc_even[...] = jnp.zeros_like(acc_even)
            acc_odd[...] = jnp.zeros_like(acc_odd)

        def pair(step, carry):
            firsts, seconds, coses, sines = [], [], [], []
            for n in range(2):
                f = 2 * step + n

                def row(ref, *where):
                    return tuple(ref[(*where, i, pl.ds(f, 1), slice(None))] for i in (0, 1))

                cy, sy_ = rotations([row(yturn, k) for k in range(turn_count(half))], half)
                coses.append(cy)
                sines.append(sy_)
                turns = [
                    rotations([row(xturn, xr, k) for k in range(turn_count(wx))], wx)
                    for xr in range(xslots)
                ]
                first, second = [], []
                for zr in range(zslots):
                    for xr in range(xslots):
                        cx, sx_ = turns[xr]
                        for c2 in range(per):
                            at = 2 * ((zcode ^ zr) * per + c2)
                            p = packed[f, pl.ds(at, 1), :]
                            q = packed[f, pl.ds(at + 1, 1), :]
                            first.append(p * cx - q * sx_)
                            second.append(p * sx_ + q * cx)
                p = packed[f, 6:7, :]
                q = packed[f, 7:8, :]
                line = lax.broadcasted_iota(jnp.int32, (16, p.shape[-1]), 0)
                one_first = jnp.zeros(line.shape, jnp.float32)
                one_second = one_first
                for xr in range(xslots):
                    cx, sx_ = row(xback, xr)
                    one_first = jnp.where(line == xr, p * cx - q * sx_, one_first)
                    one_second = jnp.where(line == xr, p * sx_ + q * cx, one_second)
                firsts.append(jnp.concatenate(first + [one_first], axis=0))
                seconds.append(jnp.concatenate(second + [one_second], axis=0))

            def product(lefts, rights):
                lh, ll = split(jnp.concatenate(lefts, axis=1))
                rh, rl = split(jnp.concatenate(rights, axis=1))
                both = dot_nt(jnp.concatenate([lh, ll], axis=0), rh)
                rows = lh.shape[0]
                return both[:rows] + dot_nt(lh, rl) + both[rows:]

            acc_even[...] += product(firsts, coses)
            acc_odd[...] += product(seconds, sines)
            return carry

        lax.fori_loop(0, freqs // 2, pair, 0, unroll=8 if closing else 4)
        if not closing:
            for copy in copies:
                copy.wait()
            return

        def slot(tile):
            code = gray(tile) ^ ycode
            place = 0
            for k in range(ybit):
                place = place * 2 + ((code >> k) & 1)
            return place

        def place(zr):
            return (keep, zr) if zr < zslots // 2 else (send, zr - zslots // 2)

        extra = xslots * per * wx
        for zr in range(zslots):
            ref, z = place(zr)
            for y in range(sy):
                ref[z, y, extra : extra + 8] = jnp.zeros((8, LANES), jnp.float32)
        at_z = (1 - (iz & 1)) * (depth - 1)
        for i, field in enumerate((0, 1, 2, 3, 4, 5, 6, 8)):
            row = field * depth
            spot = extra + 4 + i % 4
            send[0, i // 4, spot : spot + 1] = packed[
                freqs + 1 + row // 8, pl.ds(row % 8 + at_z, 1), :
            ]
        turned = 2 // per
        spare = 2 % per
        for j in range(sy // 2):
            lanes = slice(j * LANES, (j + 1) * LANES)
            up = slot(sy // 2 + j)
            down = slot(sy // 2 - 1 - j)
            at = 0
            for zr in range(zslots):
                ref, z = place(zr)
                for xr in range(xslots):
                    for c2 in range(per):
                        rows = slice(at * wx, (at + 1) * wx)
                        even = acc_even[rows, lanes] * scale
                        odd = acc_odd[rows, lanes] * scale
                        into = slice((xr * per + c2) * wx, (xr * per + c2 + 1) * wx)
                        ref[z, up, into] = even - odd
                        ref[z, down, into] = even + odd
                        at += 1
            for xr in range(xslots):
                even = acc_even[main + xr : main + xr + 1, lanes] * scale
                odd = acc_odd[main + xr : main + xr + 1, lanes] * scale
                for zr in range(zslots):
                    ref, z = place(zr)
                    ref[z, up, extra + 2 * xr : extra + 2 * xr + 1] = even - odd
                    ref[z, down, extra + 2 * xr : extra + 2 * xr + 1] = even + odd
                start = (((zcode ^ turned) * xslots + xr) * per + spare) * wx
                rows = pl.ds(pl.multiple_of(start, wx), wx)
                even = (acc_even[rows, lanes] * scale).T
                odd = (acc_odd[rows, lanes] * scale).T
                lower = slot(sy // 2 - j)
                line = slice(extra + 2 * xr + 1, extra + 2 * xr + 2)
                for zr in range(zslots):
                    ref, z = place(zr)
                    ref[z, lower, line, 0:wx] = even[0:1] + odd[0:1]
                if j < sy // 2 - 1:
                    upper = slot(sy // 2 + j + 1)
                    for zr in range(zslots):
                        ref, z = place(zr)
                        ref[z, upper, line, 0:wx] = even[LANES - 1 :] - odd[LANES - 1 :]

    return body


def near_flags(index, bits):
    low, high = [], []
    for k in range(bits):
        upper = (index >> k) & 1
        rest = index & ((1 << k) - 1)
        low.append(((upper == 1) & (rest == 0)).astype(jnp.float32))
        high.append(((upper == 0) & (rest == (1 << k) - 1)).astype(jnp.float32))
    return low, high


def weighted(flags, values):
    total = flags[0] * values[0]
    for flag, value in zip(flags[1:], values[1:]):
        total = total + flag * value
    return total


def pack_kernel(freqs, depth, wx, zbits):
    def body(*refs):
        e_in, h_in, cotangent, cosines, wavenumber, time_phase, message, waves = refs[:8]
        layers = refs[8 : 8 + zbits]
        edge, cos_near, wave_near, phase_near, sems = refs[8 + zbits :]
        upper = lax.axis_index("gx") & 1
        pairs = [
            (cotangent, message.at[0:freqs]),
            (e_in.at[:, :, 0:8], edge.at[0, 0:3]),
            (h_in.at[:, :, 0:8], edge.at[0, 3:6]),
            (e_in.at[:, :, wx - 8 : wx], edge.at[1, 0:3]),
            (h_in.at[:, :, wx - 8 : wx], edge.at[1, 3:6]),
            (cosines, cos_near),
            (wavenumber, wave_near),
            (time_phase, phase_near),
        ]
        for k, layer in enumerate(layers):
            at = (1 - ((lax.axis_index("gz") >> k) & 1)) * (depth - 1)
            pairs += [(e_in.at[:, at], layer.at[0:3]), (h_in.at[:, at], layer.at[3:6])]
        copies = [
            pltpu.make_async_copy(source, target, sems.at[i])
            for i, (source, target) in enumerate(pairs)
        ]
        for copy in copies:
            copy.start()
        for copy in copies:
            copy.wait()
        message[freqs, 0:2] = cos_near[...]
        message[freqs, 2:8] = jnp.zeros((6, LANES), jnp.float32)
        which = lax.broadcasted_iota(jnp.int32, (freqs, LANES), 0)
        for i, near in enumerate((wave_near, phase_near)):
            value = jnp.zeros((freqs, LANES), jnp.float32)
            for f in range(freqs):
                value = jnp.where(which == f, near[f], value)
            waves[i] = value
        for i in range(12):
            end = 1 - upper if i < 6 else upper
            for z in range(depth):
                row = i * depth + z
                message[freqs + 1 + row // 8, row % 8 : row % 8 + 1] = edge[
                    end, i % 6, z, pl.ds(7 * end, 1), :
                ]

    return body


def early_rows(message, freqs, depth, i):
    row = i * depth
    return message[freqs + 1 + row // 8, row % 8 : row % 8 + depth]


def column_kernel(freqs, depth, wx, wy, zbits):
    def body(*refs):
        e, h, message = refs[:3]
        zs = refs[3 : 3 + zbits]
        first, last = refs[3 + zbits :]
        low, high = near_flags(lax.axis_index("gz"), zbits)
        lane = lax.broadcasted_iota(jnp.int32, (1, LANES), 1)
        first[...] = jnp.zeros_like(first)
        last[...] = jnp.zeros_like(last)
        for i, field in enumerate((e[0], e[1], e[2], h[0], h[2])):
            turned = field.reshape(depth * wx, wy).T
            first[i : i + 1] = turned[0:1]
            last[i : i + 1] = turned[wy - 1 :]
        for i, layer in (
            (5, weighted(high, [z[1, 0:wx] for z in zs])),
            (6, weighted(low, [z[2, 0:wx] for z in zs])),
        ):
            turned = layer.T
            first[i : i + 1, 0:wx] = turned[0:1]
            last[i : i + 1, 0:wx] = turned[wy - 1 :]
        for ref, y in ((first, 0), (last, wy - 1)):
            corner = jnp.zeros((1, LANES), jnp.float32)
            side_x, side_y, next_x, next_y = (
                early_rows(message, freqs, depth, i)[:, y : y + 1] for i in (0, 1, 6, 7)
            )
            for z in range(depth):
                corner = jnp.where(lane == z, side_x[z : z + 1], corner)
                corner = jnp.where(lane == z * wx + wx - 1, side_y[z : z + 1], corner)
                corner = jnp.where(lane == depth + z, next_x[z : z + 1], corner)
                corner = jnp.where(lane == z * wx + wx - 2, next_y[z : z + 1], corner)
            ref[7:8] = corner

    return body


def total_of(terms, rows):
    value = terms[0][rows]
    for term in terms[1:]:
        value = value + term[rows]
    return value


def merge_y_kernel(count, rows, k):
    def body(*refs):
        terms, (first, last), outs = refs[:count], refs[count : count + 2], refs[count + 2 :]
        iy = lax.axis_index("gy")
        size = rows // len(outs)
        swaps = (None, k) if len(outs) == 2 else (None, k + 1, k, None)
        for i, (out, swap) in enumerate(zip(outs, swaps)):
            out[0:size] = total_of(terms, slice(i * size, (i + 1) * size))
            if swap is not None:
                upper = ((iy >> swap) & 1).astype(jnp.float32)
                out[size : size + 8] = upper * first[...] + (1.0 - upper) * last[...]

    return body


def halo_at(ref):
    rows = ref.shape[0]
    return ref[rows - 8 : rows]


def merge_x_kernel(freqs, count, rows, depth, zbits, ybits, slots, side_rows):
    def body(*refs):
        terms = refs[:count]
        message = refs[count]
        sides = refs[count + 1 : count + 1 + zbits]
        ys = refs[count + 1 + zbits : count + 1 + zbits + ybits]
        keep, out = refs[count + 2 + zbits + ybits :]
        half = (rows - 8) // 2
        size = half + 8
        keep[0:half] = total_of(terms, slice(0, half))
        out[0:half] = total_of(terms, slice(half, rows - 8))
        extra = total_of(terms, slice(rows - 8, rows))
        keep[half:size] = extra
        out[half:size] = pltpu.roll(extra, 8 - slots, 0)
        zlow, zhigh = near_flags(lax.axis_index("gz"), zbits)
        ylow, yhigh = near_flags(lax.axis_index("gy"), ybits)
        for line, i in enumerate((6, 7, 8, 10, 11)):
            row = size + line * depth
            out[row : row + depth] = early_rows(message, freqs, depth, i)
        base = size + 5 * depth

        def side(flags, i):
            ats = [rows[i] for rows in side_rows]
            return weighted(flags, [ref[at : at + 1] for at, ref in zip(ats, sides)])

        halos = [halo_at(y) for y in ys]
        out[base : base + 1] = side(zhigh, 6)
        out[base + 1 : base + 2] = side(zlow, 7)
        out[base + 2 : base + 3] = weighted(yhigh, [y[7:8] for y in halos])
        out[base + 3 : base + 4] = weighted(ylow, [y[7:8] for y in halos])

    return body


def pole_kernel():
    def body(table_in, e, pole_in, material_in, after, pole_out, base, coef_out, *scratch):
        table, pole, material, new_pole, sems = scratch
        copies = [
            pltpu.make_async_copy(source, target, sems.at[i])
            for i, (source, target) in enumerate(
                ((table_in, table), (material_in, material), (pole_in, pole))
            )
        ]
        for copy in copies:
            copy.start()
        for copy in copies:
            copy.wait()
        kind = material[...]

        def chosen(i):
            value = jnp.full(kind.shape, table[i, NPOLE - 1], jnp.float32)
            for m in range(NPOLE - 1):
                value = jnp.where(kind == m, table[i, m], value)
            return value

        decay, drive, coef = (chosen(i) for i in range(3))
        coef_out[...] = coef
        for i in range(3):
            old = pole[i]
            electric = e[i]
            new = decay * old + drive * electric
            new_pole[i] = new
            base[i] = electric - coef * (0.5 * (new + old))
        copy = pltpu.make_async_copy(new_pole, pole_out, sems.at[0])
        copy.start()
        copy.wait()

    return body


def field_kernel(freqs, depth, wx, wy, xbits, ybits, zbits, side_rows):
    def body(*refs):
        e, h, base_e, coef_ref, first, message = refs[:6]
        zs = refs[6 : 6 + zbits]
        ys = refs[6 + zbits : 6 + zbits + ybits]
        xs = [x[x.shape[0] - 5 * depth - 4 :] for x in refs[6 + zbits + ybits : 5 + zbits + ybits + xbits]]
        sides = refs[5 + zbits + ybits + xbits : 5 + 2 * zbits + ybits + xbits]
        e_out, h_out = refs[5 + 2 * zbits + ybits + xbits :]
        ix, iy, iz = (lax.axis_index(name) for name in ("gx", "gy", "gz"))
        xlow, xhigh = near_flags(ix, xbits)
        ylow, yhigh = near_flags(iy, ybits)
        zlow, zhigh = near_flags(iz, zbits)
        size = depth * wx
        base = 5 * depth
        lane = lax.broadcasted_iota(jnp.int32, (size, wy), 1)
        line = lax.broadcasted_iota(jnp.int32, (size, wy), 0) & (wx - 1)
        inside_x, inside_y, inside_z = (
            (index > 0).astype(jnp.float32) for index in (ix, iy, iz)
        )

        def flat(ref, i):
            return ref[i].reshape(size, wy)

        ex, ey, ez = (flat(e, i) for i in range(3))
        oldx, oldy, oldz = (flat(h, i) for i in range(3))

        def spread(rows):
            return jnp.broadcast_to(rows[:, None, :], (depth, wx, wy)).reshape(size, wy)

        def next_y(value, column):
            rows = value.shape[0]
            return jnp.where(lane[:rows] == wy - 1, column, pltpu.roll(value, wy - 1, 1))

        def next_x(value, rows):
            return jnp.where(line == wx - 1, spread(rows), pltpu.roll(value, size - 1, 0))

        def next_z(value, layer):
            return jnp.concatenate([value[wx:], layer], axis=0)

        def last_y(value, column):
            return jnp.where(lane == 0, column, pltpu.roll(value, 1, 1))

        def last_x(value, rows):
            return jnp.where(line == 0, spread(rows), pltpu.roll(value, 1, 0))

        def last_z(value, layer):
            return jnp.concatenate([layer, value[:-wx]], axis=0)

        ylo = weighted(ylow, [halo_at(y) for y in ys])
        yhi = weighted(yhigh, [halo_at(y) for y in ys])
        above = yhi.T

        def rows_of(flags, i):
            line = i if i < 3 else i - 1
            at = slice(line * depth, (line + 1) * depth)
            return weighted(flags, [early_rows(message, freqs, depth, i)] + [x[at] for x in xs])

        def extra_of(flags, early, i):
            return weighted(flags, [early] + [x[base + i : base + i + 1] for x in xs])

        def layer_of(flags, i):
            return weighted(flags, [z[i, 0:wx] for z in zs])

        def side_of(flags, i):
            ats = [rows[i] for rows in side_rows]
            return weighted(flags, [side[at : at + 1] for at, side in zip(ats, sides)])

        up_x, up_y = layer_of(zhigh, 0), layer_of(zhigh, 1)
        hx = oldx - courant * ((next_y(ez, above[:, 2:3]) - ez) - (next_z(ey, up_y) - ey))
        hy = oldy - courant * (
            (next_z(ex, up_x) - ex) - (next_x(ez, rows_of(xhigh, 2)) - ez)
        )
        hz = oldz - courant * (
            (next_x(ey, rows_of(xhigh, 1)) - ey) - (next_y(ex, above[:, 0:1]) - ex)
        )
        mx, my, mz = (rows_of(xlow, i) for i in range(3))
        up = jnp.concatenate([mx[1:], extra_of(xlow, side_of(zhigh, 0), 0)], axis=0)
        low_hy = rows_of(xlow, 4) - courant * ((up - mx) - (e[2, :, 0, :] - mz))
        corner = xlow[0] * above[0:depth, 7:8]
        for flag, x in zip(xlow[1:], xs):
            tail = x[base : base + 8].T
            corner = corner + flag * tail[depth : 2 * depth, 2:3]
        low_hz = rows_of(xlow, 5) - courant * (
            (e[1, :, 0, :] - my) - (next_y(mx, corner) - mx)
        )
        strip = lax.broadcasted_iota(jnp.int32, (1, LANES), 1)
        lx, ly, lz = ylo[0:1], ylo[1:2], ylo[2:3]
        up = jnp.where(
            strip >= size - wx, pltpu.roll(ylo[5:6], size - wx, 1), pltpu.roll(ly, LANES - wx, 1)
        )
        side_hx = ylo[3:4] - courant * ((first[2:3] - lz) - (up - ly))
        corner = xhigh[0] * ylo[7:8]
        for flag, x in zip(xhigh[1:], xs):
            corner = corner + flag * pltpu.roll(x[base + 3 : base + 4], 1, 1)
        right = jnp.where((strip & (wx - 1)) == wx - 1, corner, pltpu.roll(ly, LANES - 1, 1))
        side_hz = ylo[4:5] - courant * ((right - ly) - (first[0:1] - lx))
        both = jnp.concatenate([side_hx, side_hz, jnp.zeros((6, LANES), jnp.float32)], axis=0)
        both = (inside_y * both).T
        bx, by, bz = (layer_of(zlow, i) for i in range(3))
        under_hx = layer_of(zlow, 3) - courant * (
            (next_y(bz, above[0:wx, 6:7]) - bz) - (ey[:wx] - by)
        )
        right = jnp.concatenate([bz[1:], extra_of(xhigh, side_of(zlow, 2), 1)], axis=0)
        under_hy = layer_of(zlow, 4) - courant * ((ex[:wx] - bx) - (right - bz))
        under_hx = inside_z * under_hx
        under_hy = inside_z * under_hy
        low_hy = inside_x * low_hy
        low_hz = inside_x * low_hz
        curl = (
            (hz - last_y(hz, both[:, 1:2])) - (hy - last_z(hy, under_hy)),
            (hx - last_z(hx, under_hx)) - (hz - last_x(hz, low_hz)),
            (hy - last_x(hy, low_hy)) - (hx - last_y(hx, both[:, 0:1])),
        )
        coef = coef_ref[...].reshape(size, wy)
        shape = (depth, wx, wy)
        for i, magnetic in enumerate((hx, hy, hz)):
            value = flat(base_e, i) + coef * curl[i]
            h_out[i] = magnetic.reshape(shape)
            e_out[i] = value.reshape(shape)

    return body


def inject_kernel(depth, wx, wy, sy, sz, per, zcut):
    def body(*refs):
        blocks = refs[: 1 << zcut]
        e_near, h_near, coef_ref, e_out, h_out, e_new, h_new, sems = refs[1 << zcut :]
        last = depth - 1
        others = slice(0, last)
        copies = [
            pltpu.make_async_copy(e_near.at[:, others], e_out.at[:, others], sems.at[0]),
            pltpu.make_async_copy(h_near.at[:, others], h_out.at[:, others], sems.at[1]),
            pltpu.make_async_copy(h_near.at[2, last], h_out.at[2, last], sems.at[2]),
        ]
        for copy in copies:
            copy.start()
        h_copy = pltpu.make_async_copy(h_new, h_out.at[0:2, last], sems.at[3])
        e_copy = pltpu.make_async_copy(e_new, e_out.at[:, last], sems.at[4])
        ix, iy, iz = (lax.axis_index(name) for name in ("gx", "gy", "gz"))

        @pl.when(iz == sz - 1)
        def _():
            inside_x, inside_y = ((index > 0).astype(jnp.float32) for index in (ix, iy))
            lane = lax.broadcasted_iota(jnp.int32, (wx, wy), 1)
            line = lax.broadcasted_iota(jnp.int32, (wx, wy), 0)
            flip = (
                lax.broadcasted_iota(jnp.int32, (wy, wy), 0)
                + lax.broadcasted_iota(jnp.int32, (wy, wy), 1)
                == wy - 1
            ).astype(jnp.float32)
            flipped = iy < sy // 2

            def straight(value):
                turned = jnp.dot(
                    value, flip, precision=lax.Precision.HIGHEST, preferred_element_type=jnp.float32
                )
                return jnp.where(flipped, turned, value)

            tiles = [straight(ref[...]) for ref in blocks]

            def channel(c):
                start = (c % per) * wx
                return tiles[c // per][start : start + wx]

            electric_x, electric_y, magnetic_x, magnetic_y = (channel(c) for c in range(4))
            before = inside_x * tiles[3 // per][per * wx : per * wx + 1]
            beside = inside_y * blocks[2 // per][per * wx : per * wx + 8].T[0:wx, 1:2]
            last_x = jnp.where(line == 0, before, pltpu.roll(magnetic_y, 1, 0))
            last_y = jnp.where(lane == 0, beside, pltpu.roll(magnetic_x, 1, 1))
            coef = coef_ref[last]
            h_new[0] = h_near[0, last] - courant * magnetic_x
            h_new[1] = h_near[1, last] - courant * magnetic_y
            e_new[0] = e_near[0, last] + coef * (courant * magnetic_y - electric_x)
            e_new[1] = e_near[1, last] - coef * (courant * magnetic_x + electric_y)
            e_new[2] = e_near[2, last] + coef * courant * (
                (magnetic_x - last_y) - (magnetic_y - last_x)
            )

        @pl.when(iz != sz - 1)
        def _():
            for i in range(3):
                e_new[i] = e_near[i, last]
            for i in range(2):
                h_new[i] = h_near[i, last]

        h_copy.start()
        e_copy.start()
        for copy in (*copies, h_copy, e_copy):
            copy.wait()

    return body


def in_hbm(*arrays):
    return [pltpu.with_memory_space_constraint(array, pltpu.HBM) for array in arrays]


def in_vmem(*arrays):
    return [pltpu.with_memory_space_constraint(array, pltpu.VMEM) for array in arrays]


def local(
    e_field, h_field, pole_current, material, pole_table, cotangent, cosines, wavenumber, time_phase
):
    depth, wx, wy = material.shape
    sizes = sx, sy, sz = tuple(lax.axis_size(name) for name in ("gx", "gy", "gz"))
    _, _, iz = (lax.axis_index(name) for name in ("gx", "gy", "gz"))
    freqs, _, count = cotangent.shape
    scale = 1.0 / math.sqrt(freqs * count * sx * sy * sz)
    assert wy == LANES and depth * wx == LANES and 1 < sx <= 4 and sy > 1 and sz > 1
    pad = -count % LANES
    if pad:
        cotangent = jnp.pad(cotangent, ((0, 0), (0, 0), (0, pad)))
        cosines = jnp.pad(cosines, ((0, 0), (0, pad)))
    f32 = jnp.float32
    smem = pl.BlockSpec(memory_space=pltpu.SMEM)
    vmem = pl.BlockSpec(memory_space=pltpu.VMEM)
    hbm = pl.BlockSpec(memory_space=pltpu.HBM)
    small = pltpu.CompilerParams(vmem_limit_bytes=8 << 20)
    xslots = sx // 2
    zslots = min(sz, 4)
    per = 4 // zslots
    xbits, ybits, zbits = bits_of(sx), bits_of(sy), bits_of(sz)
    zcut = bits_of(zslots)

    assert 8 % depth == 0
    mine, waves, *layers = pl.pallas_call(
        pack_kernel(freqs, depth, wx, zbits),
        out_shape=[
            pltpu.VMEM((freqs + 1 + 12 * depth // 8, 8, LANES), f32),
            pltpu.VMEM((2, freqs, LANES), f32),
        ]
        + [pltpu.VMEM((6, wx, wy), f32)] * zbits,
        in_specs=[hbm] * 6,
        out_specs=[vmem] * (2 + zbits),
        scratch_shapes=[
            pltpu.VMEM((2, 6, depth, 8, LANES), f32),
            pltpu.VMEM((2, LANES), f32),
            pltpu.SMEM((freqs,), f32),
            pltpu.SMEM((freqs,), f32),
            pltpu.SemaphoreType.DMA((8 + 2 * zbits,)),
        ],
        compiler_params=small,
        name="pack",
    )(*in_hbm(e_field, h_field, cotangent, cosines, wavenumber, time_phase))
    theirs = exchange(mine, "gx", 1)
    zs = [exchange(layers[k], "gz", (2 << k) - 1) for k in range(zbits)]
    zs = in_vmem(*zs)

    half = sy * wy // 2
    width = count + pad
    block = xslots * per * wx + 8
    part_shape = pltpu.VMEM((zslots // 2, sy, block, wy), f32)
    assert freqs % 2 == 0
    sums = pltpu.VMEM((4 * xslots * wx + 16, half), f32)
    tables = [
        pltpu.VMEM((xslots, 2, freqs, width), f32),
        pltpu.VMEM((xslots, turn_count(wx), 2, freqs, width), f32),
        pltpu.VMEM((turn_count(half), 2, freqs, width), f32),
    ]
    medium = pltpu.CompilerParams(vmem_limit_bytes=24 << 20)
    waves, mine = in_vmem(waves, mine)
    *own, e_near, h_near = pl.pallas_call(
        source_kernel(freqs, depth, wx, half, sizes, zslots, xslots, scale, zbits, False),
        out_shape=(sums, sums, pltpu.VMEM(e_field.shape, f32), pltpu.VMEM(h_field.shape, f32)),
        in_specs=[vmem, vmem, hbm, hbm],
        out_specs=(vmem,) * 4,
        scratch_shapes=tables + [pltpu.SemaphoreType.DMA((2,))],
        compiler_params=medium,
        name="source_own",
    )(waves, mine, *in_hbm(e_field, h_field))
    e_near, h_near = in_vmem(e_near, h_near)
    keep, send = pl.pallas_call(
        source_kernel(freqs, depth, wx, half, sizes, zslots, xslots, scale, zbits, True),
        out_shape=(part_shape, part_shape),
        in_specs=[vmem] * (4 + zbits),
        out_specs=(vmem, vmem),
        scratch_shapes=tables + [sums, sums],
        compiler_params=medium,
        name="source_both",
    )(waves, *in_vmem(theirs, *own), *zs)

    strip = pltpu.VMEM((8, LANES), f32)
    first, last = pl.pallas_call(
        column_kernel(freqs, depth, wx, wy, zbits),
        out_shape=(strip, strip),
        in_specs=[vmem] * (3 + zbits),
        out_specs=(vmem, vmem),
        compiler_params=small,
        name="columns",
    )(e_near, h_near, *in_vmem(theirs), *zs)

    whole = jax.ShapeDtypeStruct((3, depth, wx, wy), f32)
    pole_next, base_e, coef = pl.pallas_call(
        pole_kernel(),
        out_shape=(whole, pltpu.VMEM(whole.shape, f32), pltpu.VMEM((depth, wx, wy), f32)),
        in_specs=[hbm, vmem, hbm, hbm, vmem],
        out_specs=(hbm, vmem, vmem),
        scratch_shapes=[
            pltpu.SMEM(pole_table.shape, f32),
            pltpu.VMEM(whole.shape, f32),
            pltpu.VMEM((depth, wx, wy), jnp.int32),
            pltpu.VMEM(whole.shape, f32),
            pltpu.SemaphoreType.DMA((3,)),
        ],
        compiler_params=small,
        name="pole",
    )(*in_hbm(pole_table), e_near, *in_hbm(pole_current, material), *in_vmem(first))
    base_e, coef = in_vmem(base_e, coef)

    def flat(value):
        return value.reshape(-1, LANES)

    terms = [keep, exchange(send, "gz", 1)]
    sides = [flat(terms[1])]
    side_rows = [[(i // 4) * block + block - 4 + i % 4 for i in range(8)]]
    for k in range(1, zbits):
        at = (1 - ((iz >> k) & 1)) * (depth - 1)
        rows = theirs[freqs + 1 :].reshape(12, depth, LANES)
        rows = lax.dynamic_index_in_dim(rows, at, 1, keepdims=False)
        sides.append(exchange(jnp.concatenate([rows[:7], rows[8:9]]), "gz", (2 << k) - 1))
        side_rows.append(list(range(8)))
    for k in range(1, zbits):
        part = terms[0] + terms[1]
        mask = (2 << k) - 1
        if k < zcut:
            middle = part.shape[0] // 2
            terms = [part[:middle], exchange(part[middle:], "gz", mask)]
        else:
            terms = [part, exchange(part, "gz", mask)]
    terms = [flat(term) for term in terms]
    rows = sy * block

    ys = [None] * ybits
    k = 0
    while k < ybits:
        both = k + 1 < ybits
        size = rows // 4 if both else rows // 2
        plain, laden = pltpu.VMEM((size, LANES), f32), pltpu.VMEM((size + 8, LANES), f32)
        shapes = (plain, laden, laden, plain) if both else (plain, laden)
        keep, *away = pl.pallas_call(
            merge_y_kernel(len(terms), rows, k),
            out_shape=shapes,
            in_specs=[vmem] * (len(terms) + 2),
            out_specs=(vmem,) * len(shapes),
            compiler_params=small,
            name="merge_y",
        )(*in_vmem(*terms, first, last))
        if both:
            ys[k] = exchange(away[1], "gy", (2 << k) - 1)
            other = exchange(away[2], "gy", 2 << k)
            ys[k + 1] = exchange(away[0], "gy", (4 << k) - 1)
            terms = [keep, ys[k], ys[k + 1], other]
            k += 2
        else:
            ys[k] = exchange(away[0], "gy", (2 << k) - 1)
            terms = [keep, ys[k]]
            k += 1
        rows = size
    near = [*zs, *in_vmem(*ys)]
    xs = []
    slots = xslots
    for k in range(1, xbits):
        size = (rows - 8) // 2 + 8
        keep, away = pl.pallas_call(
            merge_x_kernel(freqs, len(terms), rows, depth, zbits, ybits, slots, side_rows),
            out_shape=(
                pltpu.VMEM((size, LANES), f32),
                pltpu.VMEM((size + 5 * depth + 4, LANES), f32),
            ),
            in_specs=[vmem] * (len(terms) + 2 + zbits + ybits),
            out_specs=(vmem, vmem),
            compiler_params=small,
            name="merge_x",
        )(*in_vmem(*terms, theirs, *sides, *ys), coef)
        xs.append(exchange(away, "gx", 1 << k))
        rows = size
        slots //= 2
        terms = [keep, xs[-1]]
    part = sum(term[:rows] for term in terms)

    e_most, h_most = pl.pallas_call(
        field_kernel(freqs, depth, wx, wy, xbits, ybits, zbits, side_rows),
        out_shape=(pltpu.VMEM(whole.shape, f32), pltpu.VMEM(whole.shape, f32)),
        in_specs=[vmem] * (5 + xbits + ybits + 2 * zbits),
        out_specs=(vmem,) * 2,
        compiler_params=pltpu.CompilerParams(vmem_limit_bytes=16 << 20),
        name="fields",
    )(e_near, h_near, base_e, coef, *in_vmem(first, theirs), *near, *in_vmem(*xs, *sides))

    top = gray(sz - 1)
    blocks = [part]
    for k in reversed(range(zcut)):
        others = [exchange(value, "gz", (2 << k) - 1) for value in blocks]
        blocks = others + blocks if (top >> k) & 1 else blocks + others
    e_next, h_next = pl.pallas_call(
        inject_kernel(depth, wx, wy, sy, sz, per, zcut),
        out_shape=(whole, whole),
        in_specs=[vmem] * (len(blocks) + 3),
        out_specs=(hbm, hbm),
        scratch_shapes=[
            pltpu.VMEM((3, wx, wy), f32),
            pltpu.VMEM((2, wx, wy), f32),
            pltpu.SemaphoreType.DMA((5,)),
        ],
        compiler_params=small,
        name="inject",
    )(*in_vmem(*blocks, e_most, h_most), coef)
    return (e_next, h_next, pole_next)


def solution(mesh):
    in_specs = (
        P(None, "gz", "gx", "gy"),
        P(None, "gz", "gx", "gy"),
        P(None, "gz", "gx", "gy"),
        P("gz", "gx", "gy"),
        P(),
        P(None, None, ("gx", "gy", "gz")),
        P(None, ("gx", "gy", "gz")),
        P(),
        P(),
    )
    out_specs = (P(None, "gz", "gx", "gy"), P(None, "gz", "gx", "gy"), P(None, "gz", "gx", "gy"))
    return jax.shard_map(
        local, mesh=mesh, in_specs=in_specs, out_specs=out_specs, check_vma=False
    )
```

profile of v0, /device:TPU:1, one launch (start us, length us, event | category | flops | bytes accessed | tf_op | source)
XLA Modules:
  0.0 28.1 jit_solution(8680246375006672392)
XLA Ops:
  0.6 1.1 %pack.1 = (f32[23,8,128]{2,1,0:T(8,128)S(1)}, f32[2,16,128]{2,1,0:T(8,128)S(1)}, f32[6,32,128]{2,1,0:T(8,128)S(1)}) custom-call(f32[3,4,32,128]{3,2,1,0:T(8,128)} %refs_2_.3, f32[3,4,32,128]{3,2,1,0:T(8,128)} %refs_3_.3, f32[16,8,128]{2,1,0:T(8,128)} %refs_2_.2, f32[2,128]{1,0:T(2,128)} %refs_3_.2, f32[16]{0:T(128)} %refs_4_.1, f32[16]{0:T(128)} %refs_5_.1), custom_call_target="tpu_custom_call" | custom-call | tf_op jit(solution)/shard_map/pack/pallas_call | solution.py:700
  1.7 0.1 collective-permute-start.1
  1.8 2.8 %collective-permute-start = (f32[23,8,128]{2,1,0:T(8,128)S(1)}, f32[23,8,128]{2,1,0:T(8,128)S(1)}, u32[]{:S(2)}, u32[]{:S(2)}) collective-permute-start(f32[23,8,128]{2,1,0:T(8,128)S(1)} %get-tuple-element.28.refs_1_), channel_id=1, source_target_pairs={{0,8},{8,0},{16,24},{24,16},{1,9},{9,1},{17,25},{25,17},{2,10},{10... | collective-permute-start | bytes 282632 | tf_op jit(solution)/shard_map/ppermute | solution.py:19
  4.6 2.6 %source_own.1 = (f32[272,256]{1,0:T(8,128)S(1)}, f32[272,256]{1,0:T(8,128)S(1)}, f32[3,4,32,128]{3,2,1,0:T(8,128)S(1)}, f32[3,4,32,128]{3,2,1,0:T(8,128)S(1)}) custom-call(f32[2,16,128]{2,1,0:T(8,128)S(1)} %get-tuple-element.27.refs_0_, f32[23,8,128]{2,1,0:T(8,128)S(1)} %get-tuple-element.28.refs_1_, f32[3,4,32,128]{3,2,1,0:T(8,128)} %refs_2_.3, ...), custom_call_target="tpu_custom_call" | custom-call | tf_op jit(solution)/shard_map/source_own/pallas_call | solution.py:736
  7.2 0.4 %collective-permute-done.refs_1_.refs_2_.refs_4_.refs_5_ = f32[23,8,128]{2,1,0:T(8,128)S(1)} collective-permute-done((f32[23,8,128]{2,1,0:T(8,128)S(1)}, f32[23,8,128]{2,1,0:T(8,128)S(1)}, u32[]{:S(2)}, u32[]{:S(2)}) %collective-permute-start) | collective-permute-done | bytes 94240 | tf_op jit(solution)/shard_map/ppermute | solution.py:19
  7.6 0.0 collective-permute-done.1.refs_4_.refs_3_.refs_6_
  7.6 2.6 %source_both.1 = (f32[1,4,136,128]{3,2,1,0:T(8,128)S(1)}, f32[1,4,136,128]{3,2,1,0:T(8,128)S(1)}) custom-call(f32[2,16,128]{2,1,0:T(8,128)S(1)} %get-tuple-element.27.refs_0_, f32[23,8,128]{2,1,0:T(8,128)S(1)} %collective-permute-done.refs_1_.refs_2_.refs_4_.refs_5_, f32[272,256]{1,0:T(8,128)S(1)} %get-tuple-element.29.refs_2_, ...), custom_call_target="tpu_custom_call" | custom-call | tf_op jit(solution)/shard_map/source_both/pallas_call | solution.py:746
  10.2 0.7 %collective-permute-start.2 = (f32[1,4,136,128]{3,2,1,0:T(8,128)S(1)}, f32[1,4,136,128]{3,2,1,0:T(8,128)S(1)}, u32[]{:S(2)}, u32[]{:S(2)}) collective-permute-start(f32[1,4,136,128]{3,2,1,0:T(8,128)S(1)} %get-tuple-element.33), channel_id=1, source_target_pairs={{0,1},{1,0},{2,3},{3,2},{4,5},{5,4},{6,7},{7,6},{8,9},{9,8},{10,11... | collective-permute-start | bytes 835592 | tf_op jit(solution)/shard_map/ppermute | solution.py:19
  10.9 0.3 columns.1
  11.2 0.9 %collective-permute-done.2 = f32[1,4,136,128]{3,2,1,0:T(8,128)S(1)} collective-permute-done((f32[1,4,136,128]{3,2,1,0:T(8,128)S(1)}, f32[1,4,136,128]{3,2,1,0:T(8,128)S(1)}, u32[]{:S(2)}, u32[]{:S(2)}) %collective-permute-start.2) | collective-permute-done | bytes 278560 | tf_op jit(solution)/shard_map/ppermute | solution.py:19
  12.1 1.4 %collective-permute-start.3 = (f32[144,128]{1,0:T(8,128)S(1)}, f32[144,128]{1,0:T(8,128)S(1)}, u32[]{:S(2)}, u32[]{:S(2)}) collective-permute-start(f32[144,128]{1,0:T(8,128)S(1)} %get-tuple-element.39), channel_id=1, source_target_pairs={{0,2},{2,0},{4,6},{6,4},{1,3},{3,1},{5,7},{7,5},{8,10},{10,8},{12,... | collective-permute-start | bytes 221192 | tf_op jit(solution)/shard_map/ppermute | solution.py:19
  13.6 1.2 %collective-permute-start.4 = (f32[144,128]{1,0:T(8,128)S(1)}, f32[144,128]{1,0:T(8,128)S(1)}, u32[]{:S(2)}, u32[]{:S(2)}) collective-permute-start(f32[144,128]{1,0:T(8,128)S(1)} %get-tuple-element.40), channel_id=1, source_target_pairs={{0,6},{2,4},{4,2},{6,0},{1,7},{3,5},{5,3},{7,1},{8,14},{10,12},{12... | collective-permute-start | bytes 221192 | tf_op jit(solution)/shard_map/ppermute | solution.py:19
  14.8 0.0 collective-permute-start.5
  14.8 1.7 %pole.1 = (f32[3,4,32,128]{3,2,1,0:T(8,128)}, f32[3,4,32,128]{3,2,1,0:T(8,128)S(1)}, f32[4,32,128]{2,1,0:T(8,128)S(1)}) custom-call(f32[3,4]{1,0:T(4,128)} %table_in.1, f32[3,4,32,128]{3,2,1,0:T(8,128)S(1)} %get-tuple-element.34.refs_0_.e, f32[3,4,32,128]{3,2,1,0:T(8,128)} %pole_in.1, s32[4,32,128]{2,1,0:T(8,128)} %material_in.1, ...), custom_call_target="tpu_custom_call" | custom-call | tf_op jit(solution)/shard_map/pole/pallas_call | solution.py:767
  16.6 3.4 %collective-permute-done.5.refs_3_ = f32[136,128]{1,0:T(8,128)S(1)} collective-permute-done((f32[136,128]{1,0:T(8,128)S(1)}, f32[136,128]{1,0:T(8,128)S(1)}, u32[]{:S(2)}, u32[]{:S(2)}) %collective-permute-start.5) | collective-permute-done | bytes 69664 | tf_op jit(solution)/shard_map/ppermute | solution.py:19
  20.0 0.0 collective-permute-done.3.refs_1_.refs_6_.refs_7_
  20.0 0.0 collective-permute-done.4.refs_2_.refs_7_.refs_8_
  20.0 2.4 %collective-permute-start.6 = (f32[96,128]{1,0:T(8,128)S(1)}, f32[96,128]{1,0:T(8,128)S(1)}, u32[]{:S(2)}, u32[]{:S(2)}) collective-permute-start(f32[96,128]{1,0:T(8,128)S(1)} %get-tuple-element.44), channel_id=1, source_target_pairs={{0,16},{8,24},{16,0},{24,8},{1,17},{9,25},{17,1},{25,9},{2,18},{10... | collective-permute-start | bytes 147464 | tf_op jit(solution)/shard_map/ppermute | solution.py:19
  22.4 1.5 %collective-permute-done.6.refs_9_ = f32[96,128]{1,0:T(8,128)S(1)} collective-permute-done((f32[96,128]{1,0:T(8,128)S(1)}, f32[96,128]{1,0:T(8,128)S(1)}, u32[]{:S(2)}, u32[]{:S(2)}) %collective-permute-start.6) | collective-permute-done | bytes 49184 | tf_op jit(solution)/shard_map/ppermute | solution.py:19
  23.9 2.2 %collective-permute-start.7 = (f32[72,128]{1,0:T(8,128)S(1)}, f32[72,128]{1,0:T(8,128)S(1)}, u32[]{:S(2)}, u32[]{:S(2)}) collective-permute-start(f32[72,128]{1,0:T(8,128)S(1)} %slice_add_fusion.refs_1_), channel_id=1, source_target_pairs={{0,1},{1,0},{2,3},{3,2},{4,5},{5,4},{6,7},{7,6},{8,9},{9,8},{10,11... | collective-permute-start | bytes 110600 | tf_op jit(solution)/shard_map/ppermute | solution.py:19
  26.2 0.6 %fields.1 = (f32[3,4,32,128]{3,2,1,0:T(8,128)S(1)}, f32[3,4,32,128]{3,2,1,0:T(8,128)S(1)}) custom-call(f32[3,4,32,128]{3,2,1,0:T(8,128)S(1)} %get-tuple-element.34.refs_0_.e, f32[3,4,32,128]{3,2,1,0:T(8,128)S(1)} %get-tuple-element.35.refs_1_, f32[3,4,32,128]{3,2,1,0:T(8,128)S(1)} %get-tuple-element.45.refs_2_, ...), custom_call_target="tpu_custom_call" | custom-call | tf_op jit(solution)/shard_map/fields/pallas_call | solution.py:855
  26.8 0.3 collective-permute-done.7.refs_0_
  27.1 1.0 %inject.1 = (f32[3,4,32,128]{3,2,1,0:T(8,128)}, f32[3,4,32,128]{3,2,1,0:T(8,128)}) custom-call(f32[72,128]{1,0:T(8,128)S(1)} %collective-permute-done.7.refs_0_, f32[72,128]{1,0:T(8,128)S(1)} %slice_add_fusion.refs_1_, f32[3,4,32,128]{3,2,1,0:T(8,128)S(1)} %get-tuple-element.46.refs_2_, f32[3,4,32,128]{3,2,1,0:T(8,128)S(1)} %get-tuple-element.47.refs_3_, ...), custom_call_target="tpu_custom_call" | custom-call | tf_op jit(solution)/shard_map/inject/pallas_call | solution.py:869
  (3 shorter events, 0.1 us)
Async XLA Ops:
  1.7 5.9 %collective-permute-start.1 = (f32[6,32,128]{2,1,0:T(8,128)S(1)}, f32[6,32,128]{2,1,0:T(8,128)S(1)}, u32[]{:S(2)}, u32[]{:S(2)}) collective-permute-start(f32[6,32,128]{2,1,0:T(8,128)S(1)} %get-tuple-element.31), channel_id=1, source_target_pairs={{0,1},{1,0},{2,3},{3,2},{4,5},{5,4},{6,7},{7,6},{8,9},{9,8},{10,11... | collective-permute-start | bytes 294920 | tf_op jit(solution)/shard_map/ppermute | solution.py:19
  1.8 5.8 %collective-permute-start = (f32[23,8,128]{2,1,0:T(8,128)S(1)}, f32[23,8,128]{2,1,0:T(8,128)S(1)}, u32[]{:S(2)}, u32[]{:S(2)}) collective-permute-start(f32[23,8,128]{2,1,0:T(8,128)S(1)} %get-tuple-element.28.refs_1_), channel_id=1, source_target_pairs={{0,8},{8,0},{16,24},{24,16},{1,9},{9,1},{17,25},{25,17},{2,10},{10... | collective-permute-start | bytes 282632 | tf_op jit(solution)/shard_map/ppermute | solution.py:19
  10.2 1.9 %collective-permute-start.2 = (f32[1,4,136,128]{3,2,1,0:T(8,128)S(1)}, f32[1,4,136,128]{3,2,1,0:T(8,128)S(1)}, u32[]{:S(2)}, u32[]{:S(2)}) collective-permute-start(f32[1,4,136,128]{3,2,1,0:T(8,128)S(1)} %get-tuple-element.33), channel_id=1, source_target_pairs={{0,1},{1,0},{2,3},{3,2},{4,5},{5,4},{6,7},{7,6},{8,9},{9,8},{10,11... | collective-permute-start | bytes 835592 | tf_op jit(solution)/shard_map/ppermute | solution.py:19
  12.1 7.9 %collective-permute-start.3 = (f32[144,128]{1,0:T(8,128)S(1)}, f32[144,128]{1,0:T(8,128)S(1)}, u32[]{:S(2)}, u32[]{:S(2)}) collective-permute-start(f32[144,128]{1,0:T(8,128)S(1)} %get-tuple-element.39), channel_id=1, source_target_pairs={{0,2},{2,0},{4,6},{6,4},{1,3},{3,1},{5,7},{7,5},{8,10},{10,8},{12,... | collective-permute-start | bytes 221192 | tf_op jit(solution)/shard_map/ppermute | solution.py:19
  13.6 6.4 %collective-permute-start.4 = (f32[144,128]{1,0:T(8,128)S(1)}, f32[144,128]{1,0:T(8,128)S(1)}, u32[]{:S(2)}, u32[]{:S(2)}) collective-permute-start(f32[144,128]{1,0:T(8,128)S(1)} %get-tuple-element.40), channel_id=1, source_target_pairs={{0,6},{2,4},{4,2},{6,0},{1,7},{3,5},{5,3},{7,1},{8,14},{10,12},{12... | collective-permute-start | bytes 221192 | tf_op jit(solution)/shard_map/ppermute | solution.py:19
  14.8 5.2 %collective-permute-start.5 = (f32[136,128]{1,0:T(8,128)S(1)}, f32[136,128]{1,0:T(8,128)S(1)}, u32[]{:S(2)}, u32[]{:S(2)}) collective-permute-start(f32[136,128]{1,0:T(8,128)S(1)} %get-tuple-element.41), channel_id=1, source_target_pairs={{0,4},{2,6},{4,0},{6,2},{1,5},{3,7},{5,1},{7,3},{8,12},{10,14},{12... | collective-permute-start | bytes 208904 | tf_op jit(solution)/shard_map/ppermute | solution.py:19
  20.0 3.9 %collective-permute-start.6 = (f32[96,128]{1,0:T(8,128)S(1)}, f32[96,128]{1,0:T(8,128)S(1)}, u32[]{:S(2)}, u32[]{:S(2)}) collective-permute-start(f32[96,128]{1,0:T(8,128)S(1)} %get-tuple-element.44), channel_id=1, source_target_pairs={{0,16},{8,24},{16,0},{24,8},{1,17},{9,25},{17,1},{25,9},{2,18},{10... | collective-permute-start | bytes 147464 | tf_op jit(solution)/shard_map/ppermute | solution.py:19
  23.9 3.1 %collective-permute-start.7 = (f32[72,128]{1,0:T(8,128)S(1)}, f32[72,128]{1,0:T(8,128)S(1)}, u32[]{:S(2)}, u32[]{:S(2)}) collective-permute-start(f32[72,128]{1,0:T(8,128)S(1)} %slice_add_fusion.refs_1_), channel_id=1, source_target_pairs={{0,1},{1,0},{2,3},{3,2},{4,5},{5,4},{6,7},{7,6},{8,9},{9,8},{10,11... | collective-permute-start | bytes 110600 | tf_op jit(solution)/shard_map/ppermute | solution.py:19
where the time goes:
time: 28.4 us; the launch traced here: 28.1 us
  starting transfers between devices  10.9 us (38%)
  Pallas kernels  9.98 us (35%)
  waiting for transfers between devices  6.48 us (23%)
  between operations  0.69 us (2%)
    ppermute x8, starting transfers between devices, exchange(): lax.ppermute(array, axis, [(i, i ^ mask) for i in range(lax.axis_size(axi...  10.9 us
    ppermute x8, waiting for transfers between devices, exchange(): lax.ppermute(array, axis, [(i, i ^ mask) for i in range(lax.axis_size(axi...  6.48 us
    pallas_call x2, Pallas kernels, local(): pl.pallas_call(source_kernel(freqs, depth, wx, half, sizes, zslots, xslot...  5.23 us
    pallas_call x1, Pallas kernels, local(): pl.pallas_call(pole_kernel(), out_shape=(whole, pltpu.VMEM(whole.shape, f...  1.73 us
    pallas_call x1, Pallas kernels, local(): pl.pallas_call(pack_kernel(freqs, depth, wx, zbits), out_shape=[pltpu.VME...  1.09 us
    pallas_call x1, Pallas kernels, local(): pl.pallas_call(inject_kernel(depth, wx, wy, sy, sz, per, zcut), out_shape...  1.02 us
    pallas_call x1, Pallas kernels, local(): pl.pallas_call(field_kernel(freqs, depth, wx, wy, xbits, ybits, zbits, si...  0.6 us
  transfers between devices with their start and end apart: 8, of which 5 were waited for; matrix products, arithmetic and copies ran while one was open for 0% of the time, Pallas kernels for 19%

commit v1 on v0

--- a/solution.py
+++ b/solution.py
@@ -620,13 +620,19 @@
                 lax.broadcasted_iota(jnp.int32, (wy, wy), 0)
                 + lax.broadcasted_iota(jnp.int32, (wy, wy), 1)
                 == wy - 1
-            ).astype(jnp.float32)
+            ).astype(jnp.bfloat16)
             flipped = iy < sy // 2
 
             def straight(value):
-                turned = jnp.dot(
-                    value, flip, precision=lax.Precision.HIGHEST, preferred_element_type=jnp.float32
-                )
+                high, rest = value.astype(jnp.bfloat16), value
+                rest = rest - high.astype(jnp.float32)
+                middle = rest.astype(jnp.bfloat16)
+                low = (rest - middle.astype(jnp.float32)).astype(jnp.bfloat16)
+                parts = [
+                    jnp.dot(part, flip, preferred_element_type=jnp.float32)
+                    for part in (high, middle, low)
+                ]
+                turned = (parts[0] + parts[1]) + parts[2]
                 return jnp.where(flipped, turned, value)
 
             tiles = [straight(ref[...]) for ref in blocks]

time: 28.4 us -> 28.4 us (level)
  no operation moved by 1% of the time
where the time goes in v1:
time: 28.4 us; the launch traced here: 28 us
  starting transfers between devices  10.9 us (38%)
  Pallas kernels  9.91 us (35%)
  waiting for transfers between devices  6.48 us (23%)
  between operations  0.69 us (2%)
    ppermute x8, starting transfers between devices, exchange(): lax.ppermute(array, axis, [(i, i ^ mask) for i in range(lax.axis_size(axi...  10.9 us
    ppermute x8, waiting for transfers between devices, exchange(): lax.ppermute(array, axis, [(i, i ^ mask) for i in range(lax.axis_size(axi...  6.48 us
    pallas_call x2, Pallas kernels, local(): pl.pallas_call(source_kernel(freqs, depth, wx, half, sizes, zslots, xslot...  5.23 us
    pallas_call x1, Pallas kernels, local(): pl.pallas_call(pole_kernel(), out_shape=(whole, pltpu.VMEM(whole.shape, f...  1.73 us
    pallas_call x1, Pallas kernels, local(): pl.pallas_call(pack_kernel(freqs, depth, wx, zbits), out_shape=[pltpu.VME...  1.09 us
    pallas_call x1, Pallas kernels, local(): pl.pallas_call(inject_kernel(depth, wx, wy, sy, sz, per, zcut), out_shape...  0.95 us
    pallas_call x1, Pallas kernels, local(): pl.pallas_call(field_kernel(freqs, depth, wx, wy, xbits, ybits, zbits, si...  0.6 us
  transfers between devices with their start and end apart: 8, of which 5 were waited for; matrix products, arithmetic and copies ran while one was open for 0% of the time, Pallas kernels for 19%

profile of v1, /device:TPU:1, one launch (start us, length us, event | category | flops | bytes accessed | tf_op | source)
XLA Modules:
  0.0 28.0 jit_solution(4553451941305872940)
XLA Ops:
  0.6 1.1 %pack.1 = (f32[23,8,128]{2,1,0:T(8,128)S(1)}, f32[2,16,128]{2,1,0:T(8,128)S(1)}, f32[6,32,128]{2,1,0:T(8,128)S(1)}) custom-call(f32[3,4,32,128]{3,2,1,0:T(8,128)} %refs_2_.3, f32[3,4,32,128]{3,2,1,0:T(8,128)} %refs_3_.3, f32[16,8,128]{2,1,0:T(8,128)} %refs_2_.2, f32[2,128]{1,0:T(2,128)} %refs_3_.2, f32[16]{0:T(128)} %refs_4_.1, f32[16]{0:T(128)} %refs_5_.1), custom_call_target="tpu_custom_call" | custom-call | tf_op jit(solution)/shard_map/pack/pallas_call | solution.py:706
  1.7 0.1 collective-permute-start.1
  1.8 2.8 %collective-permute-start = (f32[23,8,128]{2,1,0:T(8,128)S(1)}, f32[23,8,128]{2,1,0:T(8,128)S(1)}, u32[]{:S(2)}, u32[]{:S(2)}) collective-permute-start(f32[23,8,128]{2,1,0:T(8,128)S(1)} %get-tuple-element.28.refs_1_), channel_id=1, source_target_pairs={{0,8},{8,0},{16,24},{24,16},{1,9},{9,1},{17,25},{25,17},{2,10},{10... | collective-permute-start | bytes 282632 | tf_op jit(solution)/shard_map/ppermute | solution.py:19
  4.6 2.6 %source_own.1 = (f32[272,256]{1,0:T(8,128)S(1)}, f32[272,256]{1,0:T(8,128)S(1)}, f32[3,4,32,128]{3,2,1,0:T(8,128)S(1)}, f32[3,4,32,128]{3,2,1,0:T(8,128)S(1)}) custom-call(f32[2,16,128]{2,1,0:T(8,128)S(1)} %get-tuple-element.27.refs_0_, f32[23,8,128]{2,1,0:T(8,128)S(1)} %get-tuple-element.28.refs_1_, f32[3,4,32,128]{3,2,1,0:T(8,128)} %refs_2_.3, ...), custom_call_target="tpu_custom_call" | custom-call | tf_op jit(solution)/shard_map/source_own/pallas_call | solution.py:742
  7.2 0.4 %collective-permute-done.refs_1_.refs_2_.refs_4_.refs_5_ = f32[23,8,128]{2,1,0:T(8,128)S(1)} collective-permute-done((f32[23,8,128]{2,1,0:T(8,128)S(1)}, f32[23,8,128]{2,1,0:T(8,128)S(1)}, u32[]{:S(2)}, u32[]{:S(2)}) %collective-permute-start) | collective-permute-done | bytes 94240 | tf_op jit(solution)/shard_map/ppermute | solution.py:19
  7.6 0.0 collective-permute-done.1.refs_4_.refs_3_.refs_6_
  7.6 2.6 %source_both.1 = (f32[1,4,136,128]{3,2,1,0:T(8,128)S(1)}, f32[1,4,136,128]{3,2,1,0:T(8,128)S(1)}) custom-call(f32[2,16,128]{2,1,0:T(8,128)S(1)} %get-tuple-element.27.refs_0_, f32[23,8,128]{2,1,0:T(8,128)S(1)} %collective-permute-done.refs_1_.refs_2_.refs_4_.refs_5_, f32[272,256]{1,0:T(8,128)S(1)} %get-tuple-element.29.refs_2_, ...), custom_call_target="tpu_custom_call" | custom-call | tf_op jit(solution)/shard_map/source_both/pallas_call | solution.py:752
  10.2 0.7 %collective-permute-start.2 = (f32[1,4,136,128]{3,2,1,0:T(8,128)S(1)}, f32[1,4,136,128]{3,2,1,0:T(8,128)S(1)}, u32[]{:S(2)}, u32[]{:S(2)}) collective-permute-start(f32[1,4,136,128]{3,2,1,0:T(8,128)S(1)} %get-tuple-element.33), channel_id=1, source_target_pairs={{0,1},{1,0},{2,3},{3,2},{4,5},{5,4},{6,7},{7,6},{8,9},{9,8},{10,11... | collective-permute-start | bytes 835592 | tf_op jit(solution)/shard_map/ppermute | solution.py:19
  10.9 0.3 columns.1
  11.2 0.9 %collective-permute-done.2 = f32[1,4,136,128]{3,2,1,0:T(8,128)S(1)} collective-permute-done((f32[1,4,136,128]{3,2,1,0:T(8,128)S(1)}, f32[1,4,136,128]{3,2,1,0:T(8,128)S(1)}, u32[]{:S(2)}, u32[]{:S(2)}) %collective-permute-start.2) | collective-permute-done | bytes 278560 | tf_op jit(solution)/shard_map/ppermute | solution.py:19
  12.1 1.4 %collective-permute-start.3 = (f32[144,128]{1,0:T(8,128)S(1)}, f32[144,128]{1,0:T(8,128)S(1)}, u32[]{:S(2)}, u32[]{:S(2)}) collective-permute-start(f32[144,128]{1,0:T(8,128)S(1)} %get-tuple-element.39), channel_id=1, source_target_pairs={{0,2},{2,0},{4,6},{6,4},{1,3},{3,1},{5,7},{7,5},{8,10},{10,8},{12,... | collective-permute-start | bytes 221192 | tf_op jit(solution)/shard_map/ppermute | solution.py:19
  13.6 1.2 %collective-permute-start.4 = (f32[144,128]{1,0:T(8,128)S(1)}, f32[144,128]{1,0:T(8,128)S(1)}, u32[]{:S(2)}, u32[]{:S(2)}) collective-permute-start(f32[144,128]{1,0:T(8,128)S(1)} %get-tuple-element.40), channel_id=1, source_target_pairs={{0,6},{2,4},{4,2},{6,0},{1,7},{3,5},{5,3},{7,1},{8,14},{10,12},{12... | collective-permute-start | bytes 221192 | tf_op jit(solution)/shard_map/ppermute | solution.py:19
  14.8 0.0 collective-permute-start.5
  14.8 1.7 %pole.1 = (f32[3,4,32,128]{3,2,1,0:T(8,128)}, f32[3,4,32,128]{3,2,1,0:T(8,128)S(1)}, f32[4,32,128]{2,1,0:T(8,128)S(1)}) custom-call(f32[3,4]{1,0:T(4,128)} %table_in.1, f32[3,4,32,128]{3,2,1,0:T(8,128)S(1)} %get-tuple-element.34.refs_0_.e, f32[3,4,32,128]{3,2,1,0:T(8,128)} %pole_in.1, s32[4,32,128]{2,1,0:T(8,128)} %material_in.1, ...), custom_call_target="tpu_custom_call" | custom-call | tf_op jit(solution)/shard_map/pole/pallas_call | solution.py:773
  16.6 3.4 %collective-permute-done.5.refs_3_ = f32[136,128]{1,0:T(8,128)S(1)} collective-permute-done((f32[136,128]{1,0:T(8,128)S(1)}, f32[136,128]{1,0:T(8,128)S(1)}, u32[]{:S(2)}, u32[]{:S(2)}) %collective-permute-start.5) | collective-permute-done | bytes 69664 | tf_op jit(solution)/shard_map/ppermute | solution.py:19
  20.0 0.0 collective-permute-done.3.refs_1_.refs_6_.refs_7_
  20.0 0.0 collective-permute-done.4.refs_2_.refs_7_.refs_8_
  20.0 2.4 %collective-permute-start.6 = (f32[96,128]{1,0:T(8,128)S(1)}, f32[96,128]{1,0:T(8,128)S(1)}, u32[]{:S(2)}, u32[]{:S(2)}) collective-permute-start(f32[96,128]{1,0:T(8,128)S(1)} %get-tuple-element.44), channel_id=1, source_target_pairs={{0,16},{8,24},{16,0},{24,8},{1,17},{9,25},{17,1},{25,9},{2,18},{10... | collective-permute-start | bytes 147464 | tf_op jit(solution)/shard_map/ppermute | solution.py:19
  22.4 1.5 %collective-permute-done.6.refs_9_ = f32[96,128]{1,0:T(8,128)S(1)} collective-permute-done((f32[96,128]{1,0:T(8,128)S(1)}, f32[96,128]{1,0:T(8,128)S(1)}, u32[]{:S(2)}, u32[]{:S(2)}) %collective-permute-start.6) | collective-permute-done | bytes 49184 | tf_op jit(solution)/shard_map/ppermute | solution.py:19
  23.9 2.2 %collective-permute-start.7 = (f32[72,128]{1,0:T(8,128)S(1)}, f32[72,128]{1,0:T(8,128)S(1)}, u32[]{:S(2)}, u32[]{:S(2)}) collective-permute-start(f32[72,128]{1,0:T(8,128)S(1)} %slice_add_fusion.refs_1_), channel_id=1, source_target_pairs={{0,1},{1,0},{2,3},{3,2},{4,5},{5,4},{6,7},{7,6},{8,9},{9,8},{10,11... | collective-permute-start | bytes 110600 | tf_op jit(solution)/shard_map/ppermute | solution.py:19
  26.2 0.6 %fields.1 = (f32[3,4,32,128]{3,2,1,0:T(8,128)S(1)}, f32[3,4,32,128]{3,2,1,0:T(8,128)S(1)}) custom-call(f32[3,4,32,128]{3,2,1,0:T(8,128)S(1)} %get-tuple-element.34.refs_0_.e, f32[3,4,32,128]{3,2,1,0:T(8,128)S(1)} %get-tuple-element.35.refs_1_, f32[3,4,32,128]{3,2,1,0:T(8,128)S(1)} %get-tuple-element.45.refs_2_, ...), custom_call_target="tpu_custom_call" | custom-call | tf_op jit(solution)/shard_map/fields/pallas_call | solution.py:861
  26.8 0.3 collective-permute-done.7.refs_0_
  27.1 0.9 %inject.1 = (f32[3,4,32,128]{3,2,1,0:T(8,128)}, f32[3,4,32,128]{3,2,1,0:T(8,128)}) custom-call(f32[72,128]{1,0:T(8,128)S(1)} %collective-permute-done.7.refs_0_, f32[72,128]{1,0:T(8,128)S(1)} %slice_add_fusion.refs_1_, f32[3,4,32,128]{3,2,1,0:T(8,128)S(1)} %get-tuple-element.46.refs_2_, f32[3,4,32,128]{3,2,1,0:T(8,128)S(1)} %get-tuple-element.47.refs_3_, ...), custom_call_target="tpu_custom_call" | custom-call | tf_op jit(solution)/shard_map/inject/pallas_call | solution.py:875
  (3 shorter events, 0.1 us)
Async XLA Ops:
  1.7 5.9 %collective-permute-start.1 = (f32[6,32,128]{2,1,0:T(8,128)S(1)}, f32[6,32,128]{2,1,0:T(8,128)S(1)}, u32[]{:S(2)}, u32[]{:S(2)}) collective-permute-start(f32[6,32,128]{2,1,0:T(8,128)S(1)} %get-tuple-element.31), channel_id=1, source_target_pairs={{0,1},{1,0},{2,3},{3,2},{4,5},{5,4},{6,7},{7,6},{8,9},{9,8},{10,11... | collective-permute-start | bytes 294920 | tf_op jit(solution)/shard_map/ppermute | solution.py:19
  1.8 5.8 %collective-permute-start = (f32[23,8,128]{2,1,0:T(8,128)S(1)}, f32[23,8,128]{2,1,0:T(8,128)S(1)}, u32[]{:S(2)}, u32[]{:S(2)}) collective-permute-start(f32[23,8,128]{2,1,0:T(8,128)S(1)} %get-tuple-element.28.refs_1_), channel_id=1, source_target_pairs={{0,8},{8,0},{16,24},{24,16},{1,9},{9,1},{17,25},{25,17},{2,10},{10... | collective-permute-start | bytes 282632 | tf_op jit(solution)/shard_map/ppermute | solution.py:19
  10.2 1.9 %collective-permute-start.2 = (f32[1,4,136,128]{3,2,1,0:T(8,128)S(1)}, f32[1,4,136,128]{3,2,1,0:T(8,128)S(1)}, u32[]{:S(2)}, u32[]{:S(2)}) collective-permute-start(f32[1,4,136,128]{3,2,1,0:T(8,128)S(1)} %get-tuple-element.33), channel_id=1, source_target_pairs={{0,1},{1,0},{2,3},{3,2},{4,5},{5,4},{6,7},{7,6},{8,9},{9,8},{10,11... | collective-permute-start | bytes 835592 | tf_op jit(solution)/shard_map/ppermute | solution.py:19
  12.1 7.9 %collective-permute-start.3 = (f32[144,128]{1,0:T(8,128)S(1)}, f32[144,128]{1,0:T(8,128)S(1)}, u32[]{:S(2)}, u32[]{:S(2)}) collective-permute-start(f32[144,128]{1,0:T(8,128)S(1)} %get-tuple-element.39), channel_id=1, source_target_pairs={{0,2},{2,0},{4,6},{6,4},{1,3},{3,1},{5,7},{7,5},{8,10},{10,8},{12,... | collective-permute-start | bytes 221192 | tf_op jit(solution)/shard_map/ppermute | solution.py:19
  13.6 6.4 %collective-permute-start.4 = (f32[144,128]{1,0:T(8,128)S(1)}, f32[144,128]{1,0:T(8,128)S(1)}, u32[]{:S(2)}, u32[]{:S(2)}) collective-permute-start(f32[144,128]{1,0:T(8,128)S(1)} %get-tuple-element.40), channel_id=1, source_target_pairs={{0,6},{2,4},{4,2},{6,0},{1,7},{3,5},{5,3},{7,1},{8,14},{10,12},{12... | collective-permute-start | bytes 221192 | tf_op jit(solution)/shard_map/ppermute | solution.py:19
  14.8 5.2 %collective-permute-start.5 = (f32[136,128]{1,0:T(8,128)S(1)}, f32[136,128]{1,0:T(8,128)S(1)}, u32[]{:S(2)}, u32[]{:S(2)}) collective-permute-start(f32[136,128]{1,0:T(8,128)S(1)} %get-tuple-element.41), channel_id=1, source_target_pairs={{0,4},{2,6},{4,0},{6,2},{1,5},{3,7},{5,1},{7,3},{8,12},{10,14},{12... | collective-permute-start | bytes 208904 | tf_op jit(solution)/shard_map/ppermute | solution.py:19
  20.0 3.9 %collective-permute-start.6 = (f32[96,128]{1,0:T(8,128)S(1)}, f32[96,128]{1,0:T(8,128)S(1)}, u32[]{:S(2)}, u32[]{:S(2)}) collective-permute-start(f32[96,128]{1,0:T(8,128)S(1)} %get-tuple-element.44), channel_id=1, source_target_pairs={{0,16},{8,24},{16,0},{24,8},{1,17},{9,25},{17,1},{25,9},{2,18},{10... | collective-permute-start | bytes 147464 | tf_op jit(solution)/shard_map/ppermute | solution.py:19
  23.9 3.1 %collective-permute-start.7 = (f32[72,128]{1,0:T(8,128)S(1)}, f32[72,128]{1,0:T(8,128)S(1)}, u32[]{:S(2)}, u32[]{:S(2)}) collective-permute-start(f32[72,128]{1,0:T(8,128)S(1)} %slice_add_fusion.refs_1_), channel_id=1, source_target_pairs={{0,1},{1,0},{2,3},{3,2},{4,5},{5,4},{6,7},{7,6},{8,9},{9,8},{10,11... | collective-permute-start | bytes 110600 | tf_op jit(solution)/shard_map/ppermute | solution.py:19
